TPU v7x, 512 devices: a whole 4x4x16 slice. The times are simulated.
512 devices in a mesh: rows: 128 (over x, z, core), rep: 4 (over y).
Axes of the slice: x: 4, y: 4, z: 16, core: 2. Of those that a mesh axis runs over, the one named last changes fastest.
Arguments:
- feats: bfloat16 [4, 32768, 512], P('rep', 'rows'), may hold values from -24 to 24
- grad_out: bfloat16 [4, 32768, 512], P('rep', 'rows'), may hold values from -6 to 6
- qkv_weight: bfloat16 [512, 1536], P('rows'), may hold values from -0.25 to 0.25
- proj_weight: bfloat16 [512, 512], P('rows'), may hold values from -0.25 to 0.25
- to_hilbert: int32 [4, 16384], P('rep', 'rows'), may hold values from 0 to 16383, as said below
- to_zorder: int32 [4, 16384], P('rep', 'rows'), may hold values from 0 to 16383, as said below
Outputs:
- grad_feats: bfloat16 [4, 32768, 512], P('rep', 'rows')
- qkv_grad: float32 [512, 1536], P('rows')
- proj_grad: float32 [512, 512], P('rows')
Inputs may be any that keep to these rules, and one draw needn't show every extreme that they name: to_hilbert[s] is a permutation of the blocks of scene s and to_zorder[s] its inverse; of the 128 Z-order blocks of one device, at most 2 have Hilbert positions on any one device, and exactly 2 for some pair of devices in every scene. `to_zorder`: the inverse of to_hilbert in every scene.
All inputs are finite; a program needn't handle non-finite values.
Results may differ from a plain program's by a relative error of at most 0.015.
The roundings to bfloat16 on the way count: a program that leaves them out, or rounds other values in their place, can miss the bound.
Values may be sent and summed in bfloat16 or wider, within the bound.
No kernel may reach another device: no remote copies, remote signals or barrier semaphores. Data moves between devices by JAX's collectives and lax.ppermute only.
A program may use at most 64 MiB of HBM per device.

v0:
```python
import jax
import jax.numpy as jnp
from jax import lax
from jax.sharding import PartitionSpec as P

HEADS = 8
CAP = 2


def from_partner(block, axis, apart):
    count = lax.axis_size(axis)
    route = []
    for low in range(count):
        high = low | 1 << apart
        if high != low and high < count:
            route += [(low, high), (high, low)]
    return lax.ppermute(block, axis, route)


def move_blocks(outgoing):
    return lax.all_to_all(outgoing, "rows", split_axis=0, concat_axis=0, tiled=True)


def rank_within(order_keys, owners):
    same_owner = owners[None, :] == owners[:, None]
    earlier = order_keys[None, :] < order_keys[:, None]
    return jnp.sum(jnp.logical_and(same_owner, earlier).astype(jnp.int32), axis=1)


def contract_rows(left, right):
    return lax.dot_general(
        left, right, (((0,), (0,)), ((), ())), preferred_element_type=jnp.float32
    )


def contract_cols(left, right):
    return lax.dot_general(
        left, right, (((1,), (1,)), ((), ())), preferred_element_type=jnp.float32
    )


def per_device(feats, grad_out, qkv_weight, proj_weight, to_hilbert, to_zorder):
    peer_count = lax.axis_size("rows")
    feature = feats[0]
    rows_dev, channels = feature.shape
    head_size = channels // HEADS
    scale = head_size ** (-0.5)
    blocks_dev = to_hilbert.shape[1]
    slot_count = peer_count * CAP
    w_qkv, w_proj = (
        lax.all_gather(qkv_weight, "rows", axis=0, tiled=True),
        lax.all_gather(proj_weight, "rows", axis=0, tiled=True),
    )
    forward_list = to_hilbert[0]
    inverse_list = to_zorder[0]
    local_ids = jnp.arange(blocks_dev, dtype=jnp.int32)
    slot_ids = jnp.arange(slot_count, dtype=jnp.int32)
    target_dev = forward_list // blocks_dev
    send_slot = target_dev * CAP + rank_within(local_ids, target_dev)
    send_table = (send_slot[None, :] == slot_ids[:, None]).astype(jnp.bfloat16)
    source_dev = inverse_list // blocks_dev
    recv_slot = source_dev * CAP + rank_within(inverse_list, source_dev)
    recv_table = (recv_slot[:, None] == slot_ids[None, :]).astype(jnp.bfloat16)
    zblocks = grad_out[0].reshape(blocks_dev, -1)
    outgoing = jnp.dot(send_table, zblocks, preferred_element_type=jnp.float32).astype(jnp.bfloat16)
    arrived = move_blocks(outgoing.reshape(peer_count, CAP, -1)).reshape(slot_count, -1)
    grad_hil = jnp.dot(recv_table, arrived, preferred_element_type=jnp.float32).astype(jnp.bfloat16)
    grad_hil = grad_hil.reshape(rows_dev, channels)
    qkv = jnp.dot(feature, w_qkv, preferred_element_type=jnp.float32).astype(jnp.bfloat16)
    query = qkv[:, :channels]
    keyval = qkv[:, channels:]
    grad_attn = contract_cols(grad_hil, w_proj).astype(jnp.bfloat16)
    other_kv = from_partner(keyval, "rows", 0)
    keys_all = jnp.concatenate([keyval[:, :channels], other_kv[:, :channels]], axis=0)
    values_all = jnp.concatenate([keyval[:, channels:], other_kv[:, channels:]], axis=0)
    attn_parts, dq_parts, dk_parts, dv_parts = ([], [], [], [])
    for head_index in range(HEADS):
        lo_col = head_index * head_size
        q_head = query[:, lo_col : lo_col + head_size]
        k_head = keys_all[:, lo_col : lo_col + head_size]
        v_head = values_all[:, lo_col : lo_col + head_size]
        g_head = grad_attn[:, lo_col : lo_col + head_size]
        score = contract_cols(q_head, k_head) * scale
        row_max = jnp.max(score, axis=1, keepdims=True)
        raised = jnp.exp(score - row_max)
        row_sum = jnp.sum(raised, axis=1, keepdims=True)
        probs = raised / row_sum
        probs_b = probs.astype(jnp.bfloat16)
        attn_parts.append(
            jnp.dot(probs_b, v_head, preferred_element_type=jnp.float32).astype(jnp.bfloat16)
        )
        dprob = contract_cols(g_head, v_head)
        delta = jnp.sum(probs * dprob, axis=1, keepdims=True)
        dscore = (probs * (dprob - delta) * scale).astype(jnp.bfloat16)
        dq_parts.append(jnp.dot(dscore, k_head, preferred_element_type=jnp.float32))
        dk_parts.append(contract_rows(dscore, q_head))
        dv_parts.append(contract_rows(probs_b, g_head))
    grad_q = jnp.concatenate(dq_parts, axis=1)
    grad_k = jnp.concatenate(dk_parts, axis=1)
    grad_v = jnp.concatenate(dv_parts, axis=1)
    other_k, other_v = (
        from_partner(grad_k[rows_dev:].astype(jnp.bfloat16), "rows", 0).astype(jnp.float32),
        from_partner(grad_v[rows_dev:].astype(jnp.bfloat16), "rows", 0).astype(jnp.float32),
    )
    grad_k = grad_k[:rows_dev] + other_k
    grad_v = grad_v[:rows_dev] + other_v
    grad_qkv = jnp.concatenate([grad_q, grad_k, grad_v], axis=1).astype(jnp.bfloat16)
    attn = jnp.concatenate(attn_parts, axis=1)
    grad_hfeat = contract_cols(grad_qkv, w_qkv).astype(jnp.bfloat16)
    hblocks = grad_hfeat.reshape(blocks_dev, -1)
    going_back = contract_rows(recv_table, hblocks).astype(jnp.bfloat16)
    returned = move_blocks(going_back.reshape(peer_count, CAP, -1)).reshape(slot_count, -1)
    grad_z = contract_rows(send_table, returned).astype(jnp.bfloat16).reshape(rows_dev, channels)
    share = channels // peer_count
    term = jnp.concatenate(
        [contract_rows(feature, grad_qkv), contract_rows(attn, grad_hil)], axis=1
    )
    total = lax.psum(term, ("rows", "rep"))
    owned = lax.dynamic_slice_in_dim(total, lax.axis_index("rows") * share, share, 0)
    return (grad_z[None], owned[:, : 3 * channels], owned[:, 3 * channels :])


def solution(mesh):
    placed = (
        P("rep", "rows", None),
        P("rep", "rows", None),
        P("rows", None),
        P("rows", None),
        P("rep", "rows"),
        P("rep", "rows"),
    )
    return jax.shard_map(
        per_device,
        mesh=mesh,
        in_specs=placed,
        out_specs=(P("rep", "rows", None), P("rows", None), P("rows", None)),
        check_vma=False,
    )
```

profile of v0, /device:TPU:2, one launch (start us, length us, event | category | flops | bytes accessed | tf_op | source)
XLA Modules:
  0.0 721.0 jit_solution(14029525855574183305)
XLA Ops:
  7.2 0.7 all-gather.4.cloned.1.call-update
  7.9 1.0 reshape_squeeze.3
  9.0 0.7 and_select_fusion.2
  9.6 0.7 fusion.202
  10.5 0.7 fusion.113
  11.5 1.0 reshape.119
  12.5 19.5 %all-to-all-start = ((bf16[128,2,1024]{2,1,0:T(2,128)(2,1)}), bf16[128,2,1024]{2,1,0:T(2,128)(2,1)S(1)}, u32[]{:S(2)}, u32[]{:S(2)}) async-start(bf16[128,2,1024]{2,1,0:T(2,128)(2,1)} %reshape.119), calls=%async_computation | async-start | bytes 1048576 | tf_op jit(solution)/shard_map/all_to_all | solution.py:21
  32.0 100.5 %all-gather.1 = bf16[128,4,512]{2,1,0:T(4,128)(2,1)S(1)} all-gather(bf16[1,4,512]{2,1,0:T(4,128)(2,1)S(1)} %bitcast.64), channel_id=1, replica_groups=mesh['rows'=128,'rep'=4] {'rows'}, dimensions={0}, use_global_device_ids=true | all-gather | bytes 528384 | tf_op jit(solution)/shard_map/all_gather | solution.py:52
  132.9 1.0 reshape.120
  133.9 22.9 %all-gather.4.cloned.1.call-done = bf16[128,4,1536]{2,1,0:T(4,128)(2,1)} async-done(((bf16[1,4,1536]{2,1,0:T(4,128)(2,1)}), bf16[128,4,1536]{2,1,0:T(4,128)(2,1)}) %all-gather.4.cloned.1.call-update) | async-done | bytes 1572880 | tf_op jit(solution)/shard_map/all_gather | solution.py:51
  156.9 2.7 reshape.126
  159.6 0.6 convolution_convert_fusion
  160.2 0.9 slice.187
  161.0 2.3 collective-permute-start
  163.4 1.0 convolution_convert_fusion.6
  164.4 1.0 reshape.121
  165.8 1.1 fusion.160
  168.6 0.4 fusion.162
  169.3 0.4 fusion.164
  170.0 0.4 fusion.166
  171.4 0.4 fusion.168
  172.0 0.4 multiply_reduce_fusion.6
  172.7 0.4 fusion.6
  174.5 0.4 multiply_reduce_fusion.4
  175.2 0.4 fusion.4
  175.8 0.3 multiply_reduce_fusion.3
  176.9 0.4 multiply_reduce_fusion.2
  177.7 0.4 fusion.2
  179.1 0.4 multiply_reduce_fusion
  180.5 2.1 collective-permute-start.2
  182.6 1.3 fusion.169
  188.6 2.4 collective-permute-start.1
  191.4 0.6 collective-permute-done.1
  192.2 1.3 convolution_convert_fusion.4
  193.6 0.6 convolution_bitcast_fusion
  194.1 1.7 reshape.122
  195.8 2.2 convolution_convert_fusion.1
  198.0 2.1 reshape.123
  200.1 12.8 %all-to-all-start.1 = ((bf16[128,2,1024]{2,1,0:T(2,128)(2,1)}), bf16[128,2,1024]{2,1,0:T(2,128)(2,1)}, u32[]{:S(2)}, u32[]{:S(2)}) async-start(bf16[128,2,1024]{2,1,0:T(2,128)(2,1)} %reshape.123), calls=%async_computation.1 | async-start | bytes 1048576 | tf_op jit(solution)/shard_map/all_to_all | solution.py:21
  212.9 3.6 pad_maximum_fusion
  216.5 29.6 %all-to-all-done.1 = bf16[128,2,1024]{2,1,0:T(2,128)(2,1)} async-done(((bf16[128,2,1024]{2,1,0:T(2,128)(2,1)}), bf16[128,2,1024]{2,1,0:T(2,128)(2,1)}, u32[]{:S(2)}, u32[]{:S(2)}) %all-to-all-start.1) | async-done | bytes 524320 | tf_op jit(solution)/shard_map/all_to_all | solution.py:21
  246.2 1.2 reshape.124
  247.7 0.8 broadcast_in_dim_reshape.3
  248.5 461.6 %all-reduce.2.cloned.1.call-done = f32[512,2048]{0,1:T(8,128)} async-done(((f32[512,2048]{0,1:T(8,128)}), f32[512,2048]{0,1:T(8,128)}) %all-reduce.2.cloned.1.call-update) | async-done | bytes 4194320 | tf_op jit(solution)/shard_map/psum | solution.py:118
  710.0 1.4 constant_dynamic-slice_fusion
  711.4 0.9 copy.13
  712.3 1.1 dynamic-slice.1
  713.4 0.7 copy.14
  (82 shorter events, 15.7 us)
Async XLA Ops:
  7.2 152.4 %copy-start = (bf16[1,256,512]{2,1,0:T(8,128)(2,1)S(1)}, bf16[1,256,512]{2,1,0:T(8,128)(2,1)}, u32[]{:S(2)}) copy-start(bf16[1,256,512]{2,1,0:T(8,128)(2,1)} %param.6) | copy-start | bytes 786436
  7.2 24.8 %copy-start.2 = (bf16[4,512]{1,0:T(4,128)(2,1)S(1)}, bf16[4,512]{1,0:T(4,128)(2,1)}, u32[]{:S(2)}) copy-start(bf16[4,512]{1,0:T(4,128)(2,1)} %param.9) | copy-start | bytes 12292
  7.2 125.5 %copy-start.3 = (s32[1,128]{1,0:T(1,128)S(1)}, s32[1,128]{1,0:T(1,128)}, u32[]{:S(2)}) copy-start(s32[1,128]{1,0:T(1,128)} %param.11) | copy-start | bytes 1540
  7.2 149.7 %all-gather.4.cloned.1.call-start = ((), (), s32[]{:S(2)}) async-start(), calls=%async_computation.3 | async-start | bytes 1585152 | tf_op jit(solution)/shard_map/all_gather | solution.py:51
  12.5 120.5 %all-to-all-start = ((bf16[128,2,1024]{2,1,0:T(2,128)(2,1)}), bf16[128,2,1024]{2,1,0:T(2,128)(2,1)S(1)}, u32[]{:S(2)}, u32[]{:S(2)}) async-start(bf16[128,2,1024]{2,1,0:T(2,128)(2,1)} %reshape.119), calls=%async_computation | async-start | bytes 1048576 | tf_op jit(solution)/shard_map/all_to_all | solution.py:21
  159.6 3.8 copy-start.1
  161.0 4.8 collective-permute-start
  180.5 11.7 %collective-permute-start.2 = (bf16[256,512]{0,1:T(8,128)(2,1)S(1)}, bf16[256,512]{0,1:T(8,128)(2,1)S(1)}, u32[]{:S(2)}, u32[]{:S(2)}) collective-permute-start(bf16[256,512]{0,1:T(8,128)(2,1)S(1)} %slice.454), channel_id=1, source_target_pairs={{0,4},{4,0},{8,12},{12,8},{16,20},{20,16},{24,28},{28,24},{32,36},... | collective-permute-start | bytes 786440 | tf_op jit(solution)/shard_map/ppermute | solution.py:17
  188.6 3.4 collective-permute-start.1
  200.1 46.1 %all-to-all-start.1 = ((bf16[128,2,1024]{2,1,0:T(2,128)(2,1)}), bf16[128,2,1024]{2,1,0:T(2,128)(2,1)}, u32[]{:S(2)}, u32[]{:S(2)}) async-start(bf16[128,2,1024]{2,1,0:T(2,128)(2,1)} %reshape.123), calls=%async_computation.1 | async-start | bytes 1048576 | tf_op jit(solution)/shard_map/all_to_all | solution.py:21
  212.9 497.2 %all-reduce.2.cloned.1.call-start = ((), (), s32[]{:S(2)}) async-start(), calls=%async_computation.2 | async-start | bytes 8388608 | tf_op jit(solution)/shard_map/psum | solution.py:118
Sparse Core Ops, SparseCore 0:
  11.1 145.7 all-gather.3
  219.2 490.8 all-reduce.1
where the time goes:
time: 722 us; the launch traced here: 721 us
  waiting for transfers between devices  515 us (71%)
  blocking collectives  101 us (14%)
  starting transfers between devices  39.3 us (5%)
  matrix products  22.5 us (3%)
  local copies, waits for them, and re-layouts  18.9 us (3%)
  between operations  14.4 us (2%)
  other arithmetic  9.94 us (1%)
    psum x1, waiting for transfers between devices, per_device(): total = lax.psum(term, ('rows', 'rep'))  462 us
    all_gather x1, blocking collectives, per_device(): lax.all_gather(proj_weight, 'rows', axis=0, tiled=True)  101 us
    all_to_all x2, starting transfers between devices, move_blocks(): lax.all_to_all(outgoing, 'rows', split_axis=0, concat_axis=0, tiled=True)  32.3 us
    all_to_all x2, waiting for transfers between devices, move_blocks(): lax.all_to_all(outgoing, 'rows', split_axis=0, concat_axis=0, tiled=True)  29.6 us
    all_gather x1, waiting for transfers between devices, per_device(): lax.all_gather(qkv_weight, 'rows', axis=0, tiled=True)  22.9 us
  transfers between devices with their start and end apart: 7, of which 4 were waited for; matrix products, arithmetic and copies ran while one was open for 3% of the time, Pallas kernels for 0%

commit v1 on v0

--- a/solution.py
+++ b/solution.py
@@ -48,7 +48,9 @@
     blocks_dev = to_hilbert.shape[1]
     slot_count = peer_count * CAP
     w_qkv, w_proj = (
-        lax.all_gather(qkv_weight, "rows", axis=0, tiled=True),
+        jnp.concatenate(
+            lax.all_to_all(jnp.stack([qkv_weight] * lax.axis_size("rows")), "rows", 0, 0), axis=0
+        ),
         lax.all_gather(proj_weight, "rows", axis=0, tiled=True),
     )
     forward_list = to_hilbert[0]

time: 722 us -> 786 us (1.089)
  blocking collectives: 101 us -> 198 us
  waiting for transfers between devices: 515 us -> 492 us
  starting transfers between devices: 39.3 us -> 28.9 us
    all_to_all x0 -> x1, blocking collectives: none -> 53 us  [move_blocks(): lax.all_to_all(outgoing, 'rows', split_axis=0, concat_axis=0, tiled=True)]
    all_gather x1, blocking collectives: 101 us -> 145 us  [per_device(): lax.all_gather(proj_weight, 'rows', axis=0, tiled=True)]
    all_gather x1 -> x0, waiting for transfers between devices: 22.9 us -> none  [per_device(): lax.all_gather(qkv_weight, 'rows', axis=0, tiled=True)]
    all_to_all x2 -> x1, starting transfers between devices: 32.3 us -> 14.7 us  [move_blocks(): lax.all_to_all(outgoing, 'rows', split_axis=0, concat_axis=0, tiled=True)]
    all_to_all x2 -> x1, waiting for transfers between devices: 29.6 us -> 29.6 us  [move_blocks(): lax.all_to_all(outgoing, 'rows', split_axis=0, concat_axis=0, tiled=True)]
  transfers between devices with their start and end apart: 7 -> 6, of which waited for: 4 -> 3; matrix products, arithmetic and copies ran while one was open for 3% -> 2% of each run, Pallas kernels for 0% -> 0%
where the time goes in v1:
time: 786 us; the launch traced here: 785 us
  waiting for transfers between devices  492 us (63%)
  blocking collectives  198 us (25%)
  starting transfers between devices  28.9 us (4%)
  matrix products  22.5 us (3%)
  local copies, waits for them, and re-layouts  19.7 us (3%)
  between operations  14.4 us (2%)
  other arithmetic  9.98 us (1%)
    psum x1, waiting for transfers between devices, per_device(): total = lax.psum(term, ('rows', 'rep'))  462 us
    all_gather x1, blocking collectives, per_device(): lax.all_gather(proj_weight, 'rows', axis=0, tiled=True)  145 us
    all_to_all x1, blocking collectives, move_blocks(): lax.all_to_all(outgoing, 'rows', split_axis=0, concat_axis=0, tiled=True)  53 us
    all_to_all x1, waiting for transfers between devices, move_blocks(): lax.all_to_all(outgoing, 'rows', split_axis=0, concat_axis=0, tiled=True)  29.6 us
  transfers between devices with their start and end apart: 6, of which 3 were waited for; matrix products, arithmetic and copies ran while one was open for 2% of the time, Pallas kernels for 0%

profile of v1, /device:TPU:2, one launch (start us, length us, event | category | flops | bytes accessed | tf_op | source)
XLA Modules:
  0.0 784.9 jit_solution(11317120249204379902)
XLA Ops:
  7.2 0.7 and_select_fusion.2
  7.9 0.7 fusion.202
  8.7 0.7 fusion.113
  9.4 1.0 reshape_squeeze.3
  11.0 53.0 %all_to_all.15 = bf16[128,2,1024]{2,1,0:T(2,128)(2,1)S(1)} all-to-all(bf16[128,2,1024]{2,1,0:T(2,128)(2,1)S(1)} %reshape.125), channel_id=1, replica_groups=mesh['rows'=128,'rep'=4] {'rows'}, dimensions={0} | all-to-all | bytes 1048576 | tf_op jit(solution)/shard_map/all_to_all | solution.py:21
  63.9 1.6 stack.2
  65.5 7.3 all-to-all-start
  72.8 144.6 %all-gather = bf16[128,4,512]{2,1,0:T(4,128)(2,1)S(1)} all-gather(bf16[1,4,512]{2,1,0:T(4,128)(2,1)S(1)} %bitcast.62), channel_id=1, replica_groups=mesh['rows'=128,'rep'=4] {'rows'}, dimensions={0}, use_global_device_ids=true | all-gather | bytes 528384 | tf_op jit(solution)/shard_map/all_gather | solution.py:54
  217.7 1.0 reshape.126
  218.7 2.7 reshape.124
  221.4 0.6 convolution_convert_fusion
  222.0 0.9 slice.187
  222.9 2.4 collective-permute-start
  225.3 1.0 convolution_convert_fusion.6
  226.3 1.0 reshape.127
  227.7 1.1 fusion.160
  230.5 0.4 fusion.162
  231.2 0.4 fusion.164
  231.9 0.4 fusion.166
  233.3 0.4 fusion.168
  233.9 0.4 multiply_reduce_fusion.6
  234.6 0.4 fusion.6
  235.2 0.3 multiply_reduce_fusion.5
  236.4 0.4 multiply_reduce_fusion.4
  237.1 0.4 fusion.4
  237.7 0.3 multiply_reduce_fusion.3
  238.8 0.4 multiply_reduce_fusion.2
  239.6 0.4 fusion.2
  241.0 0.4 multiply_reduce_fusion
  242.4 2.1 collective-permute-start.2
  244.4 1.3 fusion.169
  250.4 2.5 collective-permute-start.1
  253.3 0.5 collective-permute-done.1
  254.1 1.3 convolution_convert_fusion.4
  255.4 0.6 convolution_bitcast_fusion
  256.0 1.7 reshape.128
  257.7 2.2 convolution_convert_fusion.1
  259.8 2.1 reshape.129
  261.9 14.7 %all-to-all-start.2 = ((bf16[128,2,1024]{2,1,0:T(2,128)(2,1)}), bf16[128,2,1024]{2,1,0:T(2,128)(2,1)}, u32[]{:S(2)}, u32[]{:S(2)}) async-start(bf16[128,2,1024]{2,1,0:T(2,128)(2,1)} %reshape.129), calls=%async_computation.2 | async-start | bytes 1048576 | tf_op jit(solution)/shard_map/all_to_all | solution.py:21
  276.7 3.6 pad_maximum_fusion
  280.3 29.6 %all-to-all-done.2 = bf16[128,2,1024]{2,1,0:T(2,128)(2,1)} async-done(((bf16[128,2,1024]{2,1,0:T(2,128)(2,1)}), bf16[128,2,1024]{2,1,0:T(2,128)(2,1)}, u32[]{:S(2)}, u32[]{:S(2)}) %all-to-all-start.2) | async-done | bytes 524320 | tf_op jit(solution)/shard_map/all_to_all | solution.py:21
  309.9 1.2 reshape.130
  311.4 0.8 broadcast_in_dim_reshape.3
  312.2 461.7 %all-reduce.2.cloned.1.call-done = f32[512,2048]{0,1:T(8,128)} async-done(((f32[512,2048]{0,1:T(8,128)}), f32[512,2048]{0,1:T(8,128)}) %all-reduce.2.cloned.1.call-update) | async-done | bytes 4194320 | tf_op jit(solution)/shard_map/psum | solution.py:120
  773.9 1.4 constant_dynamic-slice_fusion
  775.3 0.9 copy.13
  776.2 1.1 dynamic-slice.1
  777.3 0.7 copy.14
  (83 shorter events, 15.5 us)
Async XLA Ops:
  7.2 214.3 %copy-start = (bf16[1,256,512]{2,1,0:T(8,128)(2,1)S(1)}, bf16[1,256,512]{2,1,0:T(8,128)(2,1)}, u32[]{:S(2)}) copy-start(bf16[1,256,512]{2,1,0:T(8,128)(2,1)} %param.6) | copy-start | bytes 786436
  10.4 53.5 %copy-start.2 = (bf16[4,1536]{1,0:T(4,128)(2,1)S(1)}, bf16[4,1536]{1,0:T(4,128)(2,1)}, u32[]{:S(2)}) copy-start(bf16[4,1536]{1,0:T(4,128)(2,1)} %param.8) | copy-start | bytes 36868
  65.5 7.3 copy-start.3
  65.5 153.2 %all-to-all-start = ((bf16[128,4,1536]{2,1,0:T(4,128)(2,1)}), bf16[128,4,1536]{2,1,0:T(4,128)(2,1)}, u32[]{:S(2)}, u32[]{:S(2)}) async-start(bf16[128,4,1536]{2,1,0:T(4,128)(2,1)} %stack.2), calls=%async_computation | async-start | bytes 3145728 | tf_op jit(solution)/shard_map/all_to_all | solution.py:52
  72.7 144.7 %copy-start.4 = (s32[1,128]{1,0:T(1,128)S(1)}, s32[1,128]{1,0:T(1,128)}, u32[]{:S(2)}) copy-start(s32[1,128]{1,0:T(1,128)} %param.11) | copy-start | bytes 1540
  221.4 3.9 copy-start.1
  222.9 4.8 collective-permute-start
  242.4 11.6 %collective-permute-start.2 = (bf16[256,512]{0,1:T(8,128)(2,1)S(1)}, bf16[256,512]{0,1:T(8,128)(2,1)S(1)}, u32[]{:S(2)}, u32[]{:S(2)}) collective-permute-start(bf16[256,512]{0,1:T(8,128)(2,1)S(1)} %slice.454), channel_id=1, source_target_pairs={{0,4},{4,0},{8,12},{12,8},{16,20},{20,16},{24,28},{28,24},{32,36},... | collective-permute-start | bytes 786440 | tf_op jit(solution)/shard_map/ppermute | solution.py:17
  250.4 3.4 collective-permute-start.1
  261.9 48.0 %all-to-all-start.2 = ((bf16[128,2,1024]{2,1,0:T(2,128)(2,1)}), bf16[128,2,1024]{2,1,0:T(2,128)(2,1)}, u32[]{:S(2)}, u32[]{:S(2)}) async-start(bf16[128,2,1024]{2,1,0:T(2,128)(2,1)} %reshape.129), calls=%async_computation.2 | async-start | bytes 1048576 | tf_op jit(solution)/shard_map/all_to_all | solution.py:21
  276.6 497.3 %all-reduce.2.cloned.1.call-start = ((), (), s32[]{:S(2)}) async-start(), calls=%async_computation.3 | async-start | bytes 8388608 | tf_op jit(solution)/shard_map/psum | solution.py:120
Sparse Core Ops, SparseCore 0:
  282.9 491.0 all-reduce.1
